TPU v7x, 512 devices: a whole 4x4x16 slice. The times are simulated.
512 devices in a mesh: wide: 128 (over x, y, z_lo, core), narrow: 4 (over z_hi).
Axes of the slice: x: 4, y: 4, z: 16 (z_hi: 4, z_lo: 4; z = z_hi * 4 + z_lo), core: 2. Of those that a mesh axis runs over, the one named last changes fastest.
Arguments:
- corr_panel: float32 [65536, 512], P('wide', 'narrow'), may hold values from -24 to 24
- factor_prev: float32 [65536, 1024], P('wide', 'narrow'), may hold values from -400 to 400
- draws_prev: float32 [1024, 512], P('narrow'), may hold values from -6 to 6
- draws_panel: float32 [512, 512], P('narrow'), may hold values from -6 to 6
- diag_inverse: float32 [512, 512], P('narrow'), may hold values from -1 to 1, as said below
Outputs:
- panel_factor: float32 [65536, 512], P('wide', 'narrow')
- smoothed: float32 [512, 65536], P(('narrow', 'wide'))
Inputs may be any that keep to these rules, and one draw needn't show every extreme that they name: `diag_inverse`: lower triangular with a positive diagonal.
All inputs are finite; a program needn't handle non-finite values.
Results may differ from a plain program's by a relative error of at most 0.0003.
Values sent between devices are 32-bit elements; how exact they have to be, the bound alone decides.
A program may use at most 64 MiB of HBM per device.

v0:
```python
import math

import jax
import jax.numpy as jnp
from jax import lax
from jax.sharding import PartitionSpec as P

PANEL = 512
ROWS_DEV = 512
WIN = 5
K = 1024


EXACT = lax.Precision.HIGHEST
HALF_ROOT = 1.0 / math.sqrt(2.0)


def broadcast(value, axis, source):
    kept = jnp.where(lax.axis_index(axis) == source, value, 0).astype(value.dtype)
    return lax.psum(kept, axis)


def contract(left_side, right_side, left_dim, right_dim):
    return lax.dot_general(
        left_side,
        right_side,
        (((left_dim,), (right_dim,)), ((), ())),
        precision=EXACT,
        preferred_element_type=jnp.float32,
    )


def smooth(uniforms):
    half_span = (WIN - 1) // 2
    feature_count = uniforms.shape[1]
    padded = jnp.pad(uniforms, ((0, 0), (half_span, half_span)))
    summed = jnp.zeros_like(uniforms)
    for offset in range(WIN):
        weight_tap = math.comb(WIN - 1, offset) / 2.0 ** (WIN - 1)
        summed = summed + weight_tap * padded[:, offset : offset + feature_count]
    return summed


def per_device(corr_panel, factor_prev, draws_prev, draws_panel, diag_inverse):
    row_count = factor_prev.shape[0]
    col_share = corr_panel.shape[1]
    narrow_place = lax.axis_index("narrow")
    pivot_block = broadcast(factor_prev, "wide", K // ROWS_DEV)
    update_part = contract(factor_prev, pivot_block, 1, 1)
    sample_part = contract(draws_prev, factor_prev, 0, 1)
    placed = lax.dynamic_update_slice_in_dim(
        jnp.zeros((row_count, PANEL), jnp.float32), corr_panel, narrow_place * col_share, 1
    )
    updated = lax.psum(placed - update_part, "narrow")
    sample_sum = lax.psum_scatter(sample_part, "narrow", scatter_dimension=0, tiled=True)
    panel_factor = contract(updated, diag_inverse, 1, 1)
    panel_part = contract(draws_panel, panel_factor, 0, 1)
    samples = sample_sum + lax.psum_scatter(panel_part, "narrow", scatter_dimension=0, tiled=True)
    own_squares = jnp.sum(factor_prev * factor_prev, axis=1) + jnp.sum(
        panel_factor * panel_factor, axis=1
    )
    variance = lax.psum(own_squares, "narrow")
    scaled = samples * lax.rsqrt(variance + 1e-06)[None, :]
    uniforms = 0.5 * (1.0 + lax.erf(scaled * HALF_ROOT))
    regrouped = lax.all_to_all(uniforms, "wide", split_axis=0, concat_axis=1, tiled=True)
    return (panel_factor, smooth(regrouped))


def solution(mesh):
    in_specs = (
        P("wide", "narrow"),
        P("wide", "narrow"),
        P("narrow", None),
        P("narrow", None),
        P("narrow", None),
    )
    out_specs = (P("wide", "narrow"), P(("narrow", "wide"), None))
    return jax.shard_map(
        per_device, mesh=mesh, in_specs=in_specs, out_specs=out_specs, check_vma=False
    )
```

profile of v0, /device:TPU:1, one launch (start us, length us, event | category | flops | bytes accessed | tf_op | source)
XLA Modules:
  0.0 1467.6 jit_solution(5167901546719474677)
XLA Ops:
  7.2 0.0 copy-start
  7.2 0.0 all-reduce.4.cloned.1.call-start
  7.2 1.9 multiply_reduce_fusion
  9.2 0.0 all-reduce.4.cloned.1.call-update
  9.2 0.0 all-reduce.6.cloned.1.call-start
  9.2 0.1 broadcast_in_dim.8
  9.4 0.8 copy-done.2
  10.2 1242.2 %all-reduce.4.cloned.1.call-done = f32[512,256]{1,0:T(8,128)} async-done(((f32[512,256]{1,0:T(8,128)}), f32[512,256]{1,0:T(8,128)}) %all-reduce.4.cloned.1.call-update) | async-done | bytes 524304 | tf_op jit(solution)/shard_map/psum | solution.py:20
  1252.5 3.1 fusion
  1255.5 0.0 all-reduce.6.cloned.1.call-update
  1255.6 0.0 reduce-scatter.2.cloned.1.call-start
  1255.6 115.5 %all-reduce.6.cloned.1.call-done = f32[512,512]{1,0:T(8,128)} async-done(((f32[512,512]{1,0:T(8,128)}), f32[512,512]{1,0:T(8,128)}) %all-reduce.6.cloned.1.call-update) | async-done | bytes 1048592 | tf_op jit(solution)/shard_map/psum | solution.py:54
  1371.2 2.4 multiply_reduce_fusion.1
  1373.6 1.0 convolution_bitcast_fusion
  1374.7 2.8 convolution_add_fusion
  1377.5 0.0 reduce-scatter.2.cloned.1.call-update
  1377.5 11.7 psum.23
  1389.2 44.5 %reduce-scatter.2.cloned.1.call-done = f32[128,512]{1,0:T(8,128)} async-done(((f32[512,512]{1,0:T(8,128)}), f32[128,512]{1,0:T(8,128)}) %reduce-scatter.2.cloned.1.call-update) | async-done | bytes 262160 | tf_op jit(solution)/shard_map/reduce_scatter | solution.py:55
  1433.8 1.0 multiply_bitcast_fusion
  1434.8 1.0 copy.10
  1435.8 9.2 all-to-all-start
  1444.9 0.8 copy.11
  1445.8 12.4 all-to-all-done
  1458.1 2.9 multiply_add_fusion
  (11 shorter events, 0.1 us)
Async XLA Ops:
  7.2 1367.5 %copy-start = (f32[256,512]{1,0:T(8,128)S(1)}, f32[256,512]{1,0:T(8,128)}, u32[]{:S(2)}) copy-start(f32[256,512]{1,0:T(8,128)} %param.7) | copy-start | bytes 1572868
  7.2 1245.3 %all-reduce.4.cloned.1.call-start = ((), (), s32[]{:S(2)}) async-start(), calls=%async_computation.2 | async-start | bytes 1048576 | tf_op jit(solution)/shard_map/psum | solution.py:20
  9.2 1362.0 %all-reduce.6.cloned.1.call-start = ((), (), s32[]{:S(2)}) async-start(), calls=%async_computation.3 | async-start | bytes 2097152 | tf_op jit(solution)/shard_map/psum | solution.py:54
  9.2 1.0 copy-start.2
  10.2 1242.3 %copy-start.1 = (f32[512,256]{1,0:T(8,128)S(1)}, f32[512,256]{1,0:T(8,128)}, u32[]{:S(2)}) copy-start(f32[512,256]{1,0:T(8,128)} %param.6) | copy-start | bytes 1572868
  1255.5 115.6 %copy-start.3 = (f32[128,512]{1,0:T(8,128)S(1)}, f32[128,512]{1,0:T(8,128)}, u32[]{:S(2)}) copy-start(f32[128,512]{1,0:T(8,128)} %param.9) | copy-start | bytes 786436
  1255.6 118.0 %copy-start.4 = (f32[128,512]{1,0:T(8,128)S(1)}, f32[128,512]{1,0:T(8,128)}, u32[]{:S(2)}) copy-start(f32[128,512]{1,0:T(8,128)} %param.8) | copy-start | bytes 786436
  1255.6 178.2 %reduce-scatter.2.cloned.1.call-start = ((), (), s32[]{:S(2)}) async-start(), calls=%async_computation.4 | async-start | bytes 1310720 | tf_op jit(solution)/shard_map/reduce_scatter | solution.py:55
  1435.8 22.4 %all-to-all-start = ((f32[128,1,512]{2,1,0:T(1,128)}), f32[128,1,512]{2,1,0:T(1,128)S(1)}, u32[]{:S(2)}, u32[]{:S(2)}) async-start(f32[128,1,512]{2,1,0:T(1,128)} %copy.10), calls=%async_computation | async-start | bytes 524288 | tf_op jit(solution)/shard_map/all_to_all | solution.py:65
Sparse Core Ops, SparseCore 0:
  10.9 1241.5 all-reduce.3
  1255.7 115.4 all-reduce.5
  1377.6 56.0 reduce-scatter.1
where the time goes:
time: 1470 us
  waiting for transfers between devices  1410 us (96%)
    psum x1, waiting for transfers between devices, broadcast(): return lax.psum(kept, axis)  1240 us
    psum x1, waiting for transfers between devices, per_device(): updated = lax.psum(placed - update_part, 'narrow')  116 us
    reduce_scatter x1, waiting for transfers between devices, per_device(): lax.psum_scatter(sample_part, 'narrow', scatter_dimension=0, tiled=True)  44.5 us
  transfers between devices with their start and end apart: 4, of which 4 were waited for; matrix products, arithmetic and copies ran while one was open for 0% of the time, Pallas kernels for 0%

commit v1 on v0

v1 whole, which is shorter than its diff:
```python
import functools
import math

import jax
import jax.numpy as jnp
from jax import lax
from jax.experimental import pallas as pl
from jax.experimental.pallas import tpu as pltpu
from jax.sharding import PartitionSpec as P

MESH = pl.DeviceIdType.MESH
EXACT = lax.Precision.HIGHEST
HALF_ROOT = 1.0 / math.sqrt(2.0)
X, Y, Z, CORES = 4, 4, 4, 2
WIDE = X * Y * Z * CORES
NARROW = 4
OWNER = 2
PLANE = X * Y * CORES


def wide_of(x, y, z, core):
    return ((x * Y + y) * Z + z) * CORES + core


def rem4(value):
    return lax.rem(value, 4)


def dot(left, right, left_dim, right_dim):
    return lax.dot_general(
        left,
        right,
        (((left_dim,), (right_dim,)), ((), ())),
        precision=EXACT,
        preferred_element_type=jnp.float32,
    )


def kernel(
    corr,
    factor,
    draws_prev,
    draws_panel,
    inverse,
    panel_out,
    smooth_out,
    f_rows,
    c_rows,
    d1,
    dv,
    piv,
    updated,
    panel,
    uni,
    mixed,
    full,
    own_sem,
    d_send,
    d_recv,
    p1_send,
    p1_recv,
    p2_send,
    p2_recv,
    f_send,
    f_recv,
    g1_send,
    g1_recv,
    g2_send,
    g2_recv,
    x_send,
    x_recv,
    q_send,
    q_recv,
    u_send,
    u_recv,
    a_send,
    a_recv,
):
    wide = lax.axis_index("wide")
    n = lax.axis_index("narrow")
    core = lax.rem(wide, CORES)
    z = rem4(lax.div(wide, CORES))
    y = rem4(lax.div(wide, CORES * Z))
    x = lax.div(wide, CORES * Z * Y)
    a = core * x + (1 - core) * y
    b = core * y + (1 - core) * x
    place = 16 * core + 4 * a + b

    def send(src, dst, send_sem, recv_sem, to_wide, to_narrow):
        copy = pltpu.make_async_remote_copy(
            src_ref=src,
            dst_ref=dst,
            send_sem=send_sem,
            recv_sem=recv_sem,
            device_id={"wide": to_wide, "narrow": to_narrow},
            device_id_type=MESH,
        )
        copy.start()
        return copy

    barrier = pltpu.get_barrier_semaphore()

    def greet(step, carry):
        pl.semaphore_signal(
            barrier,
            inc=1,
            device_id={"wide": lax.rem(wide + step, WIDE), "narrow": n},
            device_id_type=MESH,
        )
        return carry

    lax.fori_loop(1, WIDE, greet, 0)
    for k in range(1, NARROW):
        for z_other in range(Z):
            pl.semaphore_signal(
                barrier,
                inc=1,
                device_id={"wide": wide_of(x, y, z_other, core), "narrow": rem4(n + k)},
                device_id_type=MESH,
            )

    own = [
        pltpu.make_async_copy(draws_prev, d1.at[0], own_sem.at[0]),
        pltpu.make_async_copy(draws_panel, dv.at[0, 0], own_sem.at[1]),
        pltpu.make_async_copy(inverse, dv.at[1, 0], own_sem.at[2]),
        pltpu.make_async_copy(factor.at[pl.ds(128 * n, 128)], f_rows.at[0], own_sem.at[3]),
        pltpu.make_async_copy(corr.at[pl.ds(128 * n, 128)], c_rows.at[n], own_sem.at[4]),
    ]
    for copy in own:
        copy.start()
    for copy in own:
        copy.wait()
    pl.semaphore_wait(barrier, WIDE - 1 + (NARROW - 1) * Z)

    rows8 = pl.ds(8 * place, 8)
    rows8_core = pl.ds(8 * (4 * a + b), 8)
    rows16 = pl.ds(16 * place, 16)
    d_copies = []
    for k in range(1, NARROW):
        peer = rem4(n + k)
        d_copies.append(
            send(d1.at[0, rows8], d1.at[4 - k, rows8], d_send.at[k - 1, 0], d_recv.at[k - 1, 0], wide, peer)
        )
        d_copies.append(
            send(
                dv.at[core, 0, rows8_core],
                dv.at[core, 4 - k, rows8_core],
                d_send.at[k - 1, 1],
                d_recv.at[k - 1, 1],
                wide,
                peer,
            )
        )

    @pl.when(wide == OWNER)
    def _():
        copies = []
        for to in range(1, PLANE):
            to_core, to_a, to_b = to // 16, (to // 4) % 4, to % 4
            to_x, to_y = (to_a, to_b) if to_core else (to_b, to_a)
            rows = pl.ds(16 * to, 16)
            copies.append(
                send(
                    factor.at[rows],
                    piv.at[0, rows],
                    p1_send.at[to],
                    p1_recv,
                    wide_of(to_x, to_y, 1, to_core),
                    n,
                )
            )
        local = pltpu.make_async_copy(factor.at[pl.ds(0, 16)], piv.at[0, pl.ds(0, 16)], p1_send.at[0])
        local.start()
        local.wait()
        for copy in copies:
            copy.wait_send()

    @pl.when((z == 1) & (wide != OWNER))
    def _():
        pltpu.make_async_copy(piv.at[0, rows16], piv.at[0, rows16], p1_recv).wait()

    @pl.when(z == 1)
    def _():
        copies = []
        for k in range(NARROW):
            slot = rem4(4 - k)
            for z_other in range(Z):
                if k == 0 and z_other == 1:
                    continue
                copies.append(
                    send(
                        piv.at[0, rows16],
                        piv.at[(4 - k) % 4, rows16],
                        p2_send.at[k, z_other],
                        p2_recv.at[(4 - k) % 4],
                        wide_of(x, y, z_other, core),
                        rem4(n + k),
                    )
                )
        for copy in copies:
            copy.wait_send()

    f_copies = []
    for k in (2, 1, 3):
        peer = rem4(n + k)
        rows = pl.ds(128 * peer, 128)
        f_copies.append(
            (
                send(factor.at[rows], f_rows.at[4 - k], f_send.at[k - 1, 0], f_recv.at[k - 1, 0], wide, peer),
                send(corr.at[rows], c_rows.at[n], f_send.at[k - 1, 1], f_recv.at[k - 1, 1], wide, peer),
            )
        )

    for copy in d_copies:
        copy.wait()
    for slot in range(1, NARROW):
        pltpu.make_async_copy(piv.at[slot, rows16], piv.at[slot, rows16], p2_recv.at[slot]).wait()

    @pl.when(z != 1)
    def _():
        pltpu.make_async_copy(piv.at[0, rows16], piv.at[0, rows16], p2_recv.at[0]).wait()

    def pieces(first, count, at_core):
        in_core = first - 16 * at_core
        return (
            d1.at[pl.ds(1, 3), pl.ds(8 * first, 8 * count)],
            dv.at[at_core, pl.ds(1, 3), pl.ds(8 * in_core, 8 * count)],
            piv.at[:, pl.ds(16 * first, 16 * count)],
        )

    def along(step, use_y):
        return wide_of(rem4(x + step * (1 - use_y)), rem4(y + step * use_y), z, core)

    first_copies = []
    for step in (1, 3, 2):
        for kind, ref in enumerate(pieces(place, 1, core)):
            first_copies.append(
                send(ref, ref, g1_send.at[step - 1, kind], g1_recv.at[step - 1, kind], along(step, core), n)
            )
    for copy in first_copies:
        copy.wait()

    partner = wide_of(x, y, z, 1 - core)

    def to_partner(group, index):
        copies = []
        for kind, ref in enumerate(pieces(16 * core + 4 * group, 4, core)):
            copies.append(send(ref, ref, x_send.at[index, kind], x_recv.at[index, kind], partner, n))
        return copies

    second_copies = []
    for step in (1, 3, 2):
        for kind, ref in enumerate(pieces(16 * core + 4 * a, 4, core)):
            second_copies.append(
                send(ref, ref, g2_send.at[step - 1, kind], g2_recv.at[step - 1, kind], along(step, 1 - core), n)
            )
    core_copies = to_partner(a, 0)
    for order, step in enumerate((1, 3, 2)):
        for kind in range(3):
            second_copies[3 * order + kind].wait_recv()
        core_copies += to_partner(rem4(a + 4 - step), step)
    for copy in second_copies:
        copy.wait_send()
    for copy in core_copies:
        copy.wait()

    for pair in f_copies:
        for copy in pair:
            copy.wait()

    product = jnp.zeros((128, 512), jnp.float32)
    for k in range(NARROW):
        product = product + dot(f_rows[k], piv[k], 1, 1)
    for m in range(NARROW):
        updated[:, 128 * m : 128 * m + 128] = c_rows[m] - product[:, 128 * m : 128 * m + 128]
    squares = jnp.zeros((128, 1), jnp.float32)
    new = updated[...]
    for k in range(NARROW):
        value = dot(new, dv[1, k], 1, 1)
        panel[k] = value
        squares = squares + jnp.sum(value * value, axis=1, keepdims=True)
    q_copies = []
    for k in (2, 1, 3):
        q_copies.append(
            send(
                panel.at[k],
                panel_out.at[pl.ds(128 * n, 128)],
                q_send.at[k - 1],
                q_recv.at[k - 1],
                wide,
                rem4(n + k),
            )
        )
    panel_out[pl.ds(pl.multiple_of(128 * n, 128), 128), :] = panel[0]

    sums = jnp.zeros((128, 512), jnp.float32)
    for k in range(NARROW):
        part = f_rows[k]
        squares = squares + jnp.sum(part * part, axis=1, keepdims=True)
        sums = sums + dot(part, d1[k], 1, 0) + dot(panel[k], dv[0, k], 1, 0)
    scaled = sums * lax.rsqrt(squares + 1e-06)
    uniforms = 0.5 * (1.0 + lax.erf(scaled * HALF_ROOT))
    for m in range(NARROW):
        uni[m] = uniforms[:, 128 * m : 128 * m + 128].T.reshape(128, 1, 128)

    u_copies = []
    for k in (2, 1, 3):
        peer = rem4(n + k)
        u_copies.append(send(uni.at[peer], mixed.at[:, n], u_send.at[k - 1], u_recv.at[k - 1], wide, peer))
    local = pltpu.make_async_copy(uni.at[n], mixed.at[:, n], own_sem.at[0])
    local.start()
    local.wait()
    for copy in u_copies:
        copy.wait()

    mine = pl.ds(4 + 4 * wide, 4)

    def hand_out(step, carry):
        to = lax.rem(wide + step, WIDE)
        pltpu.make_async_remote_copy(
            src_ref=mixed.at[to],
            dst_ref=full.at[mine],
            send_sem=a_send,
            recv_sem=a_recv,
            device_id={"wide": to, "narrow": n},
            device_id_type=MESH,
        ).start()
        return carry

    lax.fori_loop(1, WIDE, hand_out, 0)
    local = pltpu.make_async_copy(mixed.at[wide], full.at[mine], own_sem.at[1])
    local.start()
    full[3] = jnp.zeros((1, 128), jnp.float32)
    full[516] = jnp.zeros((1, 128), jnp.float32)
    local.wait()
    for copy in q_copies:
        copy.wait()
    all_rows = pl.ds(4, 4 * (WIDE - 1))
    pltpu.make_async_copy(full.at[all_rows], full.at[all_rows], a_recv).wait()
    pltpu.make_async_copy(full.at[all_rows], full.at[all_rows], a_send).wait()

    before = full[3:515].reshape(512, 128)
    now = full[4:516].reshape(512, 128)
    after = full[5:517].reshape(512, 128)
    lane = lax.broadcasted_iota(jnp.int32, (512, 128), 1)
    total = 6.0 / 16.0 * now
    for shift, weight in ((1, 4.0 / 16.0), (2, 1.0 / 16.0)):
        left = jnp.where(lane < shift, pltpu.roll(before, shift, 1), pltpu.roll(now, shift, 1))
        right = jnp.where(lane >= 128 - shift, pltpu.roll(after, 128 - shift, 1), pltpu.roll(now, 128 - shift, 1))
        total = total + weight * (left + right)
    smooth_out[...] = total


def per_device(corr_panel, factor_prev, draws_prev, draws_panel, diag_inverse):
    anywhere = pl.BlockSpec(memory_space=pl.ANY)
    vmem = pl.BlockSpec(memory_space=pltpu.VMEM)
    dma = pltpu.SemaphoreType.DMA
    panel_factor, smoothed = pl.pallas_call(
        kernel,
        name="panel",
        out_shape=(
            jax.ShapeDtypeStruct((512, 128), jnp.float32),
            jax.ShapeDtypeStruct((512, 128), jnp.float32),
        ),
        in_specs=[anywhere] * 5,
        out_specs=(vmem, vmem),
        scratch_shapes=[
            pltpu.VMEM((4, 128, 256), jnp.float32),
            pltpu.VMEM((4, 128, 128), jnp.float32),
            pltpu.VMEM((4, 256, 512), jnp.float32),
            pltpu.VMEM((2, 4, 128, 512), jnp.float32),
            pltpu.VMEM((4, 512, 256), jnp.float32),
            pltpu.VMEM((128, 512), jnp.float32),
            pltpu.VMEM((4, 128, 128), jnp.float32),
            pltpu.VMEM((4, 128, 1, 128), jnp.float32),
            pltpu.VMEM((128, 4, 1, 128), jnp.float32),
            pltpu.VMEM((520, 1, 128), jnp.float32),
            dma((5,)),
            dma((3, 2)),
            dma((3, 2)),
            dma((PLANE,)),
            dma,
            dma((4, 4)),
            dma((4,)),
            dma((3, 2)),
            dma((3, 2)),
            dma((3, 3)),
            dma((3, 3)),
            dma((3, 3)),
            dma((3, 3)),
            dma((4, 3)),
            dma((4, 3)),
            dma((3,)),
            dma((3,)),
            dma((3,)),
            dma((3,)),
            dma,
            dma,
        ],
        compiler_params=pltpu.CompilerParams(
            collective_id=0, has_side_effects=True, vmem_limit_bytes=48 * 2**20
        ),
    )(corr_panel, factor_prev, draws_prev, draws_panel, diag_inverse)
    return panel_factor, smoothed.reshape(1, 512 * 128)


def solution(mesh):
    in_specs = (
        P("wide", "narrow"),
        P("wide", "narrow"),
        P("narrow", None),
        P("narrow", None),
        P("narrow", None),
    )
    out_specs = (P("wide", "narrow"), P(("narrow", "wide"), None))
    return jax.shard_map(
        per_device, mesh=mesh, in_specs=in_specs, out_specs=out_specs, check_vma=False
    )
```

time: 1470 us -> 134 us (0.09)
  waiting for transfers between devices: 1410 us -> 0 us
  Pallas kernels: 0 us -> 127 us
    psum x2 -> x0, waiting for transfers between devices: 1360 us -> none  [the longest x1 1240 us: broadcast(): return lax.psum(kept, axis)]
    pallas_call x0 -> x1, Pallas kernels: none -> 127 us  [per_device(): pl.pallas_call(kernel, name='panel', out_shape=(jax.ShapeDtypeStruct((512...]
    reduce_scatter x1 -> x0, waiting for transfers between devices: 44.5 us -> none  [per_device(): lax.psum_scatter(sample_part, 'narrow', scatter_dimension=0, tiled=True)]
  transfers between devices with their start and end apart: 4 -> 0, of which waited for: 4 -> 0; matrix products, arithmetic and copies ran while one was open for 0% -> 0% of each run, Pallas kernels for 0% -> 0%
where the time goes in v1:
time: 134 us
  Pallas kernels  127 us (95%)
  local copies, waits for them, and re-layouts  6.33 us (5%)
    pallas_call x1, Pallas kernels, per_device(): pl.pallas_call(kernel, name='panel', out_shape=(jax.ShapeDtypeStruct((512...  127 us
    unnamed x12, local copies, waits for them, and re-layouts  6.33 us

profile of v1, /device:TPU:1, one launch (start us, length us, event | category | flops | bytes accessed | tf_op | source)
XLA Modules:
  0.0 133.5 jit_solution(15476051468936644693)
XLA Ops:
  0.6 0.0 copy-start
  0.6 1.0 copy-done
  1.7 0.0 copy-start.1
  1.7 1.0 copy-done.1
  2.7 0.0 copy-start.2
  2.7 0.9 copy-done.2
  3.7 0.0 copy-start.3
  3.7 0.9 copy-done.3
  4.6 0.0 copy-start.4
  4.6 0.9 copy-done.4
  5.6 126.5 %panel.1 = (f32[512,128]{1,0:T(8,128)S(1)}, f32[512,128]{1,0:T(8,128)S(1)}) custom-call(f32[512,128]{1,0:T(8,128)S(1)} %copy-done.2, f32[512,256]{1,0:T(8,128)S(1)} %copy-done, f32[256,512]{1,0:T(8,128)S(1)} %copy-done.1, f32[128,512]{1,0:T(8,128)S(1)} %copy-done.3, f32[128,512]{1,0:T(8,128)S(1)} %copy-done.4), custom_call_target="tpu_custom_call" | custom-call | tf_op jit(solution)/shard_map/panel/pallas_call | solution.py:358
  132.1 0.7 copy.9
  132.8 0.7 copy.10
Async XLA Ops:
  0.6 1.0 copy-start
  1.7 1.0 copy-start.1
  2.7 0.9 copy-start.2
  3.7 0.9 copy-start.3
  4.6 0.9 copy-start.4

commit v2 on v1

v2 whole, which is shorter than its diff:
```python
import functools
import math

import jax
import jax.numpy as jnp
from jax import lax
from jax.experimental import pallas as pl
from jax.experimental.pallas import tpu as pltpu
from jax.sharding import PartitionSpec as P

MESH = pl.DeviceIdType.MESH
HALF_ROOT = 1.0 / math.sqrt(2.0)
X, Y, Z, CORES = 4, 4, 4, 2
WIDE = X * Y * Z * CORES
NARROW = 4
OWNER = 2
PLANE = X * Y * CORES


def wide_of(x, y, z, core):
    return ((x * Y + y) * Z + z) * CORES + core


def rem4(value):
    return lax.rem(value, 4)


def dot(left, right, left_dim, right_dim):
    return lax.dot_general(
        left,
        right,
        (((left_dim,), (right_dim,)), ((), ())),
        preferred_element_type=jnp.float32,
    )


def split(value):
    head = value.astype(jnp.bfloat16)
    return head, (value - head.astype(jnp.float32)).astype(jnp.bfloat16)


def dot3(left, right, left_dim, right_dim):
    return dot(left[0], right[0], left_dim, right_dim) + (
        dot(left[0], right[1], left_dim, right_dim) + dot(left[1], right[0], left_dim, right_dim)
    )


def kernel(
    corr,
    factor,
    draws_prev,
    draws_panel,
    inverse,
    panel_out,
    smooth_out,
    f_rows,
    c_rows,
    d1,
    dv,
    piv,
    d1_split,
    dv_split,
    piv_split,
    updated,
    panel,
    uni,
    mixed,
    full,
    own_sem,
    d_send,
    d_recv,
    p1_send,
    p1_recv,
    p2_send,
    p2_recv,
    f_send,
    f_recv,
    g1_send,
    g1_recv,
    g2_send,
    g2_recv,
    x_send,
    x_recv,
    q_send,
    q_recv,
    u_send,
    u_recv,
    a_send,
    a_recv,
):
    wide = lax.axis_index("wide")
    n = lax.axis_index("narrow")
    core = lax.rem(wide, CORES)
    z = rem4(lax.div(wide, CORES))
    y = rem4(lax.div(wide, CORES * Z))
    x = lax.div(wide, CORES * Z * Y)
    a = core * x + (1 - core) * y
    b = core * y + (1 - core) * x
    place = 16 * core + 4 * a + b
    column = x * Y + y
    flat = column * CORES + core
    height = n * Z + z

    def in_plane(step):
        to = lax.rem(flat + step, PLANE)
        to_column, to_core = lax.div(to, CORES), lax.rem(to, CORES)
        return to, to_column, to_core, (to_column * Z + z) * CORES + to_core

    def in_ring(step):
        to = lax.rem(height + step, Z * NARROW)
        to_n, to_z = lax.div(to, Z), lax.rem(to, Z)
        return to, to_n, to_z, (column * Z + to_z) * CORES + core

    def remote(src, dst, send_sem, recv_sem, to_wide, to_narrow):
        return pltpu.make_async_remote_copy(
            src_ref=src,
            dst_ref=dst,
            send_sem=send_sem,
            recv_sem=recv_sem,
            device_id={"wide": to_wide, "narrow": to_narrow},
            device_id_type=MESH,
        )

    def send(*what):
        copy = remote(*what)
        copy.start()
        return copy

    barrier = pltpu.get_barrier_semaphore()

    def greet_ring(step, carry):
        _, to_n, _, to_wide = in_ring(step)
        pl.semaphore_signal(
            barrier, inc=1, device_id={"wide": to_wide, "narrow": to_n}, device_id_type=MESH
        )
        return carry

    def greet_plane(step, carry):
        _, _, _, to_wide = in_plane(step)
        pl.semaphore_signal(
            barrier, inc=1, device_id={"wide": to_wide, "narrow": n}, device_id_type=MESH
        )
        return carry

    lax.fori_loop(1, Z * NARROW, greet_ring, 0)
    lax.fori_loop(1, PLANE, greet_plane, 0)

    own = [
        pltpu.make_async_copy(draws_prev, d1.at[0], own_sem.at[0]),
        pltpu.make_async_copy(draws_panel, dv.at[0, 0], own_sem.at[1]),
        pltpu.make_async_copy(inverse, dv.at[1, 0], own_sem.at[2]),
        pltpu.make_async_copy(factor.at[pl.ds(128 * n, 128)], f_rows.at[0], own_sem.at[3]),
        pltpu.make_async_copy(corr.at[pl.ds(128 * n, 128)], c_rows.at[n], own_sem.at[4]),
    ]
    for copy in own:
        copy.start()
    for copy in own:
        copy.wait()
    pl.semaphore_wait(barrier, Z * NARROW - 1 + PLANE - 1)

    rows8 = pl.ds(8 * place, 8)
    rows8_core = pl.ds(8 * (4 * a + b), 8)
    rows16 = pl.ds(16 * place, 16)
    d_copies = []
    for k in (2, 1, 3):
        peer = rem4(n + k)
        d_copies.append(
            send(d1.at[0, rows8], d1.at[4 - k, rows8], d_send.at[k - 1, 0], d_recv.at[k - 1, 0], wide, peer)
        )
        d_copies.append(
            send(
                dv.at[core, 0, rows8_core],
                dv.at[core, 4 - k, rows8_core],
                d_send.at[k - 1, 1],
                d_recv.at[k - 1, 1],
                wide,
                peer,
            )
        )

    def to_plane(to):
        to_core, to_a, to_b = to // 16, (to // 4) % 4, to % 4
        to_x, to_y = (to_a, to_b) if to_core else (to_b, to_a)
        rows = pl.ds(16 * to, 16)
        return remote(
            factor.at[rows], piv.at[0, rows], p1_send.at[to], p1_recv, wide_of(to_x, to_y, 1, to_core), n
        )

    @pl.when(wide == OWNER)
    def _():
        for to in range(1, PLANE):
            to_plane(to).start()
        local = pltpu.make_async_copy(factor.at[pl.ds(0, 16)], piv.at[0, pl.ds(0, 16)], p1_send.at[0])
        local.start()
        local.wait()

    @pl.when((z == 1) & (wide != OWNER))
    def _():
        pltpu.make_async_copy(piv.at[0, rows16], piv.at[0, rows16], p1_recv).wait()

    def along_z(k, z_other):
        return remote(
            piv.at[0, rows16],
            piv.at[(4 - k) % 4, rows16],
            p2_send.at[k, z_other],
            p2_recv.at[(4 - k) % 4],
            wide_of(x, y, z_other, core),
            rem4(n + k),
        )

    others = [(k, z_other) for k in (2, 1, 3, 0) for z_other in range(Z) if (k, z_other) != (0, 1)]

    @pl.when(z == 1)
    def _():
        for k, z_other in others:
            along_z(k, z_other).start()

    def piece(kind, first, count):
        if kind == 0:
            return d1.at[pl.ds(1, 3), pl.ds(8 * first, 8 * count)]
        if kind == 1:
            return dv.at[core, pl.ds(1, 3), pl.ds(8 * (first - 16 * core), 8 * count)]
        return piv.at[:, pl.ds(16 * first, 16 * count)]

    def along(step, use_y):
        return wide_of(rem4(x + step * (1 - use_y)), rem4(y + step * use_y), z, core)

    def gather_first(kind):
        ref = piece(kind, place, 1)
        return [
            send(ref, ref, g1_send.at[step - 1, kind], g1_recv.at[step - 1, kind], along(step, core), n)
            for step in (1, 3, 2)
        ]

    partner = wide_of(x, y, z, 1 - core)

    def to_partner(kind, group, index):
        ref = piece(kind, 16 * core + 4 * group, 4)
        return send(ref, ref, x_send.at[index, kind], x_recv.at[index, kind], partner, n)

    def gather_second(kind):
        ref = piece(kind, 16 * core + 4 * a, 4)
        return [
            send(ref, ref, g2_send.at[step - 1, kind], g2_recv.at[step - 1, kind], along(step, 1 - core), n)
            for step in (1, 3, 2)
        ]

    for copy in d_copies:
        copy.wait_recv()
    first_d = [gather_first(0), gather_first(1)]
    for slot in range(1, NARROW):
        pltpu.make_async_copy(piv.at[slot, rows16], piv.at[slot, rows16], p2_recv.at[slot]).wait()

    @pl.when(z != 1)
    def _():
        pltpu.make_async_copy(piv.at[0, rows16], piv.at[0, rows16], p2_recv.at[0]).wait()

    f_copies, c_copies = {}, {}
    for k in (2, 1, 3):
        peer = rem4(n + k)
        rows = pl.ds(128 * peer, 128)
        c_copies[k] = send(corr.at[rows], c_rows.at[n], f_send.at[k - 1, 1], f_recv.at[k - 1, 1], wide, peer)
        f_copies[k] = send(
            factor.at[rows], f_rows.at[4 - k], f_send.at[k - 1, 0], f_recv.at[k - 1, 0], wide, peer
        )
    first_p = gather_first(2)

    second, core_copies = [], []
    for kind in (0, 1):
        for copy in first_d[kind]:
            copy.wait()
        second.append(gather_second(kind))
        core_copies.append(to_partner(kind, a, 0))
    for copy in first_p:
        copy.wait()
    second.append(gather_second(2))
    core_copies.append(to_partner(2, a, 0))
    for kind in range(3):
        for order, step in enumerate((1, 3, 2)):
            second[kind][order].wait_recv()
            core_copies.append(to_partner(kind, rem4(a + 4 - step), step))
    for copy in d_copies:
        copy.wait_send()
    for copies in second:
        for copy in copies:
            copy.wait_send()
    for copy in core_copies:
        copy.wait()

    @pl.when(wide == OWNER)
    def _():
        for to in range(1, PLANE):
            to_plane(to).wait_send()

    @pl.when(z == 1)
    def _():
        for k, z_other in others:
            along_z(k, z_other).wait_send()

    for k in range(NARROW):
        piv_split[0, k], piv_split[1, k] = split(piv[k])
        d1_split[0, k], d1_split[1, k] = split(d1[k])
        for which in range(2):
            dv_split[0, which, k], dv_split[1, which, k] = split(dv[which, k])

    product = jnp.zeros((128, 512), jnp.float32)
    sums = jnp.zeros((128, 512), jnp.float32)
    squares = jnp.zeros((128, 1), jnp.float32)
    for k in (0, 1, 3, 2):
        if k:
            f_copies[4 - k].wait_recv()
        part = f_rows[k]
        squares = squares + jnp.sum(part * part, axis=1, keepdims=True)
        part = split(part)
        product = product + dot3(part, (piv_split[0, k], piv_split[1, k]), 1, 1)
        sums = sums + dot3(part, (d1_split[0, k], d1_split[1, k]), 1, 0)
    for k in (1, 3, 2):
        c_copies[k].wait_recv()
    for m in range(NARROW):
        updated[:, 128 * m : 128 * m + 128] = c_rows[m] - product[:, 128 * m : 128 * m + 128]
    new = split(updated[...])
    for k in range(NARROW):
        value = dot3(new, (dv_split[0, 1, k], dv_split[1, 1, k]), 1, 1)
        panel[k] = value
        squares = squares + jnp.sum(value * value, axis=1, keepdims=True)
        sums = sums + dot3(split(value), (dv_split[0, 0, k], dv_split[1, 0, k]), 1, 0)
    scaled = sums * lax.rsqrt(squares + 1e-06)
    uniforms = 0.5 * (1.0 + lax.erf(scaled * HALF_ROOT))
    for m in range(NARROW):
        uni[m] = uniforms[:, 128 * m : 128 * m + 128].T.reshape(X * Y, Z, CORES, 1, 128)

    def up(step, carry):
        to, to_n, to_z, to_wide = in_ring(lax.rem(7 * step, Z * NARROW))
        remote(
            uni.at[to_n, :, to_z], mixed.at[:, :, z, n], u_send.at[to], u_recv.at[height], to_wide, to_n
        ).start()
        return carry

    lax.fori_loop(1, Z * NARROW, up, 0)
    q_copies = []
    for k in (2, 1, 3):
        q_copies.append(
            send(
                panel.at[k],
                panel_out.at[pl.ds(128 * n, 128)],
                q_send.at[k - 1],
                q_recv.at[k - 1],
                wide,
                rem4(n + k),
            )
        )
    local = pltpu.make_async_copy(uni.at[n, :, z], mixed.at[:, :, z, n], own_sem.at[0])
    local.start()
    panel_out[pl.ds(pl.multiple_of(128 * n, 128), 128), :] = panel[0]
    local.wait()

    def up_done(step, carry):
        to, to_n, to_z, to_wide = in_ring(step)
        copy = remote(
            uni.at[to_n, :, to_z], mixed.at[:, :, to_z, to_n], u_send.at[to], u_recv.at[to], to_wide, to_n
        )
        copy.wait()
        return carry

    lax.fori_loop(1, Z * NARROW, up_done, 0)

    def hand_out(step, carry):
        to, to_column, to_core, to_wide = in_plane(step)
        remote(
            mixed.at[to_column, to_core], full.at[column, :, core], a_send.at[to], a_recv.at[flat], to_wide, n
        ).start()
        return carry

    lax.fori_loop(1, PLANE, hand_out, 0)
    local = pltpu.make_async_copy(mixed.at[column, core], full.at[column, :, core], own_sem.at[1])
    local.start()
    local.wait()

    def handed(step, carry):
        to, to_column, to_core, to_wide = in_plane(step)
        remote(
            mixed.at[to_column, to_core],
            full.at[to_column, :, to_core],
            a_send.at[to],
            a_recv.at[to],
            to_wide,
            n,
        ).wait()
        return carry

    lax.fori_loop(1, PLANE, handed, 0)

    now = full[...].reshape(512, 128)
    row = lax.broadcasted_iota(jnp.int32, (512, 128), 0)
    lane = lax.broadcasted_iota(jnp.int32, (512, 128), 1)
    before = jnp.where(row == 0, 0.0, pltpu.roll(now, 1, 0))
    after = jnp.where(row == 511, 0.0, pltpu.roll(now, 511, 0))
    total = 6.0 / 16.0 * now
    for shift, weight in ((1, 4.0 / 16.0), (2, 1.0 / 16.0)):
        left = jnp.where(lane < shift, pltpu.roll(before, shift, 1), pltpu.roll(now, shift, 1))
        right = jnp.where(lane >= 128 - shift, pltpu.roll(after, 128 - shift, 1), pltpu.roll(now, 128 - shift, 1))
        total = total + weight * (left + right)
    smooth_out[...] = total
    for k in (1, 2, 3):
        f_copies[k].wait_send()
        c_copies[k].wait_send()
    for copy in q_copies:
        copy.wait()


def per_device(corr_panel, factor_prev, draws_prev, draws_panel, diag_inverse):
    anywhere = pl.BlockSpec(memory_space=pl.ANY)
    vmem = pl.BlockSpec(memory_space=pltpu.VMEM)
    dma = pltpu.SemaphoreType.DMA
    panel_factor, smoothed = pl.pallas_call(
        kernel,
        name="panel",
        out_shape=(
            jax.ShapeDtypeStruct((512, 128), jnp.float32),
            jax.ShapeDtypeStruct((512, 128), jnp.float32),
        ),
        in_specs=[anywhere] * 5,
        out_specs=(vmem, vmem),
        scratch_shapes=[
            pltpu.VMEM((4, 128, 256), jnp.float32),
            pltpu.VMEM((4, 128, 128), jnp.float32),
            pltpu.VMEM((4, 256, 512), jnp.float32),
            pltpu.VMEM((2, 4, 128, 512), jnp.float32),
            pltpu.VMEM((4, 512, 256), jnp.float32),
            pltpu.VMEM((2, 4, 256, 512), jnp.bfloat16),
            pltpu.VMEM((2, 2, 4, 128, 512), jnp.bfloat16),
            pltpu.VMEM((2, 4, 512, 256), jnp.bfloat16),
            pltpu.VMEM((128, 512), jnp.float32),
            pltpu.VMEM((4, 128, 128), jnp.float32),
            pltpu.VMEM((4, X * Y, Z, CORES, 1, 128), jnp.float32),
            pltpu.VMEM((X * Y, CORES, Z, NARROW, 1, 128), jnp.float32),
            pltpu.VMEM((X * Y, Z, CORES, NARROW, 1, 128), jnp.float32),
            dma((5,)),
            dma((3, 2)),
            dma((3, 2)),
            dma((PLANE,)),
            dma,
            dma((4, 4)),
            dma((4,)),
            dma((3, 2)),
            dma((3, 2)),
            dma((3, 3)),
            dma((3, 3)),
            dma((3, 3)),
            dma((3, 3)),
            dma((4, 3)),
            dma((4, 3)),
            dma((3,)),
            dma((3,)),
            dma((16,)),
            dma((16,)),
            dma((PLANE,)),
            dma((PLANE,)),
        ],
        compiler_params=pltpu.CompilerParams(
            collective_id=0, has_side_effects=True, vmem_limit_bytes=67043328
        ),
    )(corr_panel, factor_prev, draws_prev, draws_panel, diag_inverse)
    return panel_factor, smoothed.reshape(1, 512 * 128)


def solution(mesh):
    in_specs = (
        P("wide", "narrow"),
        P("wide", "narrow"),
        P("narrow", None),
        P("narrow", None),
        P("narrow", None),
    )
    out_specs = (P("wide", "narrow"), P(("narrow", "wide"), None))
    return jax.shard_map(
        per_device, mesh=mesh, in_specs=in_specs, out_specs=out_specs, check_vma=False
    )
```

time: 134 us -> 105 us (0.78)
  Pallas kernels: 127 us -> 101 us
  local copies, waits for them, and re-layouts: 6.33 us -> 2.42 us
    pallas_call x1, Pallas kernels: 127 us -> 101 us  [per_device(): pl.pallas_call(kernel, name='panel', out_shape=(jax.ShapeDtypeStruct((512...]
    unnamed x12 -> x4, local copies, waits for them, and re-layouts: 6.33 us -> 2.42 us
where the time goes in v2:
time: 105 us; the launch traced here: 104 us
  Pallas kernels  101 us (96%)
  local copies, waits for them, and re-layouts  2.42 us (2%)
    pallas_call x1, Pallas kernels, per_device(): pl.pallas_call(kernel, name='panel', out_shape=(jax.ShapeDtypeStruct((512...  101 us
    unnamed x4, local copies, waits for them, and re-layouts  2.42 us

profile of v2, /device:TPU:1, one launch (start us, length us, event | category | flops | bytes accessed | tf_op | source)
XLA Modules:
  0.0 103.8 jit_solution(6550445505220278975)
XLA Ops:
  0.6 100.8 %panel.1 = (f32[512,128]{1,0:T(8,128)}, f32[512,128]{1,0:T(8,128)}) custom-call(f32[512,128]{1,0:T(8,128)} %corr.1, f32[512,256]{1,0:T(8,128)} %factor.1, f32[256,512]{1,0:T(8,128)} %draws_prev.1, f32[128,512]{1,0:T(8,128)} %draws_panel.1, f32[128,512]{1,0:T(8,128)} %inverse.1), custom_call_target="tpu_custom_call" | custom-call | tf_op jit(solution)/shard_map/panel/pallas_call | solution.py:415
  101.4 0.0 copy-start
  101.4 1.7 %copy.9 = f32[512,128]{1,0:T(8,128)} copy(f32[512,128]{1,0:T(8,128)} %get-tuple-element.8) | data formatting | bytes 524288
  103.1 0.0 copy-done
  103.1 0.7 copy.10
Async XLA Ops:
  101.4 1.7 %copy-start = (f32[512,128]{1,0:T(8,128)S(1)}, f32[512,128]{1,0:T(8,128)}, u32[]{:S(2)}) copy-start(f32[512,128]{1,0:T(8,128)} %get-tuple-element.5) | copy-start | bytes 786436

commit v3 on v2

--- a/solution.py
+++ b/solution.py
@@ -66,6 +66,7 @@
     uni,
     mixed,
     full,
+    result,
     own_sem,
     d_send,
     d_recv,
@@ -126,25 +127,6 @@
         copy.start()
         return copy
 
-    barrier = pltpu.get_barrier_semaphore()
-
-    def greet_ring(step, carry):
-        _, to_n, _, to_wide = in_ring(step)
-        pl.semaphore_signal(
-            barrier, inc=1, device_id={"wide": to_wide, "narrow": to_n}, device_id_type=MESH
-        )
-        return carry
-
-    def greet_plane(step, carry):
-        _, _, _, to_wide = in_plane(step)
-        pl.semaphore_signal(
-            barrier, inc=1, device_id={"wide": to_wide, "narrow": n}, device_id_type=MESH
-        )
-        return carry
-
-    lax.fori_loop(1, Z * NARROW, greet_ring, 0)
-    lax.fori_loop(1, PLANE, greet_plane, 0)
-
     own = [
         pltpu.make_async_copy(draws_prev, d1.at[0], own_sem.at[0]),
         pltpu.make_async_copy(draws_panel, dv.at[0, 0], own_sem.at[1]),
@@ -154,9 +136,24 @@
     ]
     for copy in own:
         copy.start()
+
+    barrier = pltpu.get_barrier_semaphore()
+
+    def greet(to_wide, to_n):
+        pl.semaphore_signal(
+            barrier, inc=1, device_id={"wide": to_wide, "narrow": to_n}, device_id_type=MESH
+        )
+
+    turned = [[rem4(at + step) for step in range(4)] for at in (x, y, z, n)]
+    for step in range(1, Z * NARROW):
+        greet(wide_of(x, y, turned[2][step % 4], core), turned[3][step // 4])
+    for step in range(1, PLANE):
+        greet(
+            wide_of(turned[0][step // 8], turned[1][step // 2 % 4], z, core if step % 2 == 0 else 1 - core), n
+        )
+    pl.semaphore_wait(barrier, Z * NARROW - 1 + PLANE - 1)
     for copy in own:
         copy.wait()
-    pl.semaphore_wait(barrier, Z * NARROW - 1 + PLANE - 1)
 
     rows8 = pl.ds(8 * place, 8)
     rows8_core = pl.ds(8 * (4 * a + b), 8)
@@ -165,7 +162,14 @@
     for k in (2, 1, 3):
         peer = rem4(n + k)
         d_copies.append(
-            send(d1.at[0, rows8], d1.at[4 - k, rows8], d_send.at[k - 1, 0], d_recv.at[k - 1, 0], wide, peer)
+            send(
+                d1.at[0, rows8],
+                d1.at[4 - k, rows8],
+                d_send.at[k - 1, 0],
+                d_recv.at[k - 1, 0],
+                wide,
+                peer,
+            )
         )
         d_copies.append(
             send(
@@ -178,6 +182,17 @@
             )
         )
 
+    def trade(k, kind):
+        peer = rem4(n + k)
+        rows = pl.ds(128 * peer, 128)
+        src, dst = (factor.at[rows], f_rows.at[4 - k]) if kind == 0 else (corr.at[rows], c_rows.at[n])
+        return remote(src, dst, f_send.at[k - 1, kind], f_recv.at[k - 1, kind], wide, peer)
+
+    @pl.when(z != 1)
+    def _():
+        for k in (2, 1, 3):
+            trade(k, 1).start()
+
     def to_plane(to):
         to_core, to_a, to_b = to // 16, (to // 4) % 4, to % 4
         to_x, to_y = (to_a, to_b) if to_core else (to_b, to_a)
@@ -214,6 +229,8 @@
     def _():
         for k, z_other in others:
             along_z(k, z_other).start()
+        for k in (2, 1, 3):
+            trade(k, 1).start()
 
     def piece(kind, first, count):
         if kind == 0:
@@ -255,14 +272,10 @@
     def _():
         pltpu.make_async_copy(piv.at[0, rows16], piv.at[0, rows16], p2_recv.at[0]).wait()
 
-    f_copies, c_copies = {}, {}
+    f_copies = {k: trade(k, 0) for k in (2, 1, 3)}
+    c_copies = {k: trade(k, 1) for k in (2, 1, 3)}
     for k in (2, 1, 3):
-        peer = rem4(n + k)
-        rows = pl.ds(128 * peer, 128)
-        c_copies[k] = send(corr.at[rows], c_rows.at[n], f_send.at[k - 1, 1], f_recv.at[k - 1, 1], wide, peer)
-        f_copies[k] = send(
-            factor.at[rows], f_rows.at[4 - k], f_send.at[k - 1, 0], f_recv.at[k - 1, 0], wide, peer
-        )
+        f_copies[k].start()
     first_p = gather_first(2)
 
     second, core_copies = [], []
@@ -319,11 +332,13 @@
     for m in range(NARROW):
         updated[:, 128 * m : 128 * m + 128] = c_rows[m] - product[:, 128 * m : 128 * m + 128]
     new = split(updated[...])
+    inverse_split = tuple(dv_split[part, 1].reshape(512, 512) for part in range(2))
+    draws_split = tuple(dv_split[part, 0].reshape(512, 512) for part in range(2))
+    value = dot3(new, inverse_split, 1, 1)
     for k in range(NARROW):
-        value = dot3(new, (dv_split[0, 1, k], dv_split[1, 1, k]), 1, 1)
-        panel[k] = value
-        squares = squares + jnp.sum(value * value, axis=1, keepdims=True)
-        sums = sums + dot3(split(value), (dv_split[0, 0, k], dv_split[1, 0, k]), 1, 0)
+        panel[k] = value[:, 128 * k : 128 * k + 128]
+    squares = squares + jnp.sum(value * value, axis=1, keepdims=True)
+    sums = sums + dot3(split(value), draws_split, 1, 0)
     scaled = sums * lax.rsqrt(squares + 1e-06)
     uniforms = 0.5 * (1.0 + lax.erf(scaled * HALF_ROOT))
     for m in range(NARROW):
@@ -337,21 +352,18 @@
         return carry
 
     lax.fori_loop(1, Z * NARROW, up, 0)
-    q_copies = []
-    for k in (2, 1, 3):
-        q_copies.append(
-            send(
-                panel.at[k],
-                panel_out.at[pl.ds(128 * n, 128)],
-                q_send.at[k - 1],
-                q_recv.at[k - 1],
-                wide,
-                rem4(n + k),
-            )
-        )
+    q_copies = {
+        k: remote(
+            panel.at[k], panel_out.at[pl.ds(128 * n, 128)], q_send.at[k - 1], q_recv.at[k - 1], wide, rem4(n + k)
+        )
+        for k in (1, 2, 3)
+    }
+    q_copies[1].start()
+    q_copies[3].start()
     local = pltpu.make_async_copy(uni.at[n, :, z], mixed.at[:, :, z, n], own_sem.at[0])
     local.start()
-    panel_out[pl.ds(pl.multiple_of(128 * n, 128), 128), :] = panel[0]
+    kept = pltpu.make_async_copy(panel.at[0], panel_out.at[pl.ds(128 * n, 128)], own_sem.at[2])
+    kept.start()
     local.wait()
 
     def up_done(step, carry):
@@ -372,6 +384,7 @@
         return carry
 
     lax.fori_loop(1, PLANE, hand_out, 0)
+    q_copies[2].start()
     local = pltpu.make_async_copy(mixed.at[column, core], full.at[column, :, core], own_sem.at[1])
     local.start()
     local.wait()
@@ -400,17 +413,20 @@
         left = jnp.where(lane < shift, pltpu.roll(before, shift, 1), pltpu.roll(now, shift, 1))
         right = jnp.where(lane >= 128 - shift, pltpu.roll(after, 128 - shift, 1), pltpu.roll(now, 128 - shift, 1))
         total = total + weight * (left + right)
-    smooth_out[...] = total
+    result[...] = total
+    done = pltpu.make_async_copy(result, smooth_out, own_sem.at[3])
+    done.start()
     for k in (1, 2, 3):
         f_copies[k].wait_send()
         c_copies[k].wait_send()
-    for copy in q_copies:
-        copy.wait()
+    for k in (1, 2, 3):
+        q_copies[k].wait()
+    kept.wait()
+    done.wait()
 
 
 def per_device(corr_panel, factor_prev, draws_prev, draws_panel, diag_inverse):
     anywhere = pl.BlockSpec(memory_space=pl.ANY)
-    vmem = pl.BlockSpec(memory_space=pltpu.VMEM)
     dma = pltpu.SemaphoreType.DMA
     panel_factor, smoothed = pl.pallas_call(
         kernel,
@@ -420,7 +436,7 @@
             jax.ShapeDtypeStruct((512, 128), jnp.float32),
         ),
         in_specs=[anywhere] * 5,
-        out_specs=(vmem, vmem),
+        out_specs=(anywhere, anywhere),
         scratch_shapes=[
             pltpu.VMEM((4, 128, 256), jnp.float32),
             pltpu.VMEM((4, 128, 128), jnp.float32),
@@ -435,6 +451,7 @@
             pltpu.VMEM((4, X * Y, Z, CORES, 1, 128), jnp.float32),
             pltpu.VMEM((X * Y, CORES, Z, NARROW, 1, 128), jnp.float32),
             pltpu.VMEM((X * Y, Z, CORES, NARROW, 1, 128), jnp.float32),
+            pltpu.VMEM((512, 128), jnp.float32),
             dma((5,)),
             dma((3, 2)),
             dma((3, 2)),

time: 105 us -> 99.9 us (0.951)
  Pallas kernels: 101 us -> 96 us
    pallas_call x1, Pallas kernels: 101 us -> 96 us  [per_device(): pl.pallas_call(kernel, name='panel', out_shape=(jax.ShapeDtypeStruct((512...]
where the time goes in v3:
time: 99.9 us; the launch traced here: 99.1 us
  Pallas kernels  96 us (96%)
  local copies, waits for them, and re-layouts  2.42 us (2%)
    pallas_call x1, Pallas kernels, per_device(): pl.pallas_call(kernel, name='panel', out_shape=(jax.ShapeDtypeStruct((512...  96 us
    unnamed x4, local copies, waits for them, and re-layouts  2.42 us

profile of v3, /device:TPU:1, one launch (start us, length us, event | category | flops | bytes accessed | tf_op | source)
XLA Modules:
  0.0 99.1 jit_solution(15083234362258442264)
XLA Ops:
  0.6 96.0 %panel.1 = (f32[512,128]{1,0:T(8,128)}, f32[512,128]{1,0:T(8,128)}) custom-call(f32[512,128]{1,0:T(8,128)} %corr.1, f32[512,256]{1,0:T(8,128)} %factor.1, f32[256,512]{1,0:T(8,128)} %draws_prev.1, f32[128,512]{1,0:T(8,128)} %draws_panel.1, f32[128,512]{1,0:T(8,128)} %inverse.1), custom_call_target="tpu_custom_call" | custom-call | tf_op jit(solution)/shard_map/panel/pallas_call | solution.py:431
  96.6 0.0 copy-start
  96.6 1.7 %copy.9 = f32[512,128]{1,0:T(8,128)} copy(f32[512,128]{1,0:T(8,128)} %get-tuple-element.8) | data formatting | bytes 524288
  98.3 0.0 copy-done
  98.3 0.7 copy.10
Async XLA Ops:
  96.6 1.7 %copy-start = (f32[512,128]{1,0:T(8,128)S(1)}, f32[512,128]{1,0:T(8,128)}, u32[]{:S(2)}) copy-start(f32[512,128]{1,0:T(8,128)} %get-tuple-element.5) | copy-start | bytes 786436

commit v4 on v3

--- a/solution.py
+++ b/solution.py
@@ -62,6 +62,7 @@
     dv_split,
     piv_split,
     updated,
+    flat_uni,
     panel,
     uni,
     mixed,
@@ -184,28 +185,31 @@
 
     def trade(k, kind):
         peer = rem4(n + k)
-        rows = pl.ds(128 * peer, 128)
-        src, dst = (factor.at[rows], f_rows.at[4 - k]) if kind == 0 else (corr.at[rows], c_rows.at[n])
+        if kind < 2:
+            src = factor.at[pl.ds(128 * peer + 64 * kind, 64)]
+            dst = f_rows.at[4 - k, pl.ds(64 * kind, 64)]
+        else:
+            src, dst = corr.at[pl.ds(128 * peer, 128)], c_rows.at[n]
         return remote(src, dst, f_send.at[k - 1, kind], f_recv.at[k - 1, kind], wide, peer)
 
     @pl.when(z != 1)
     def _():
         for k in (2, 1, 3):
-            trade(k, 1).start()
+            trade(k, 2).start()
 
     def to_plane(to):
         to_core, to_a, to_b = to // 16, (to // 4) % 4, to % 4
         to_x, to_y = (to_a, to_b) if to_core else (to_b, to_a)
         rows = pl.ds(16 * to, 16)
         return remote(
-            factor.at[rows], piv.at[0, rows], p1_send.at[to], p1_recv, wide_of(to_x, to_y, 1, to_core), n
+            factor.at[rows], piv.at[0, rows], p1_send, p1_recv, wide_of(to_x, to_y, 1, to_core), n
         )
 
     @pl.when(wide == OWNER)
     def _():
         for to in range(1, PLANE):
             to_plane(to).start()
-        local = pltpu.make_async_copy(factor.at[pl.ds(0, 16)], piv.at[0, pl.ds(0, 16)], p1_send.at[0])
+        local = pltpu.make_async_copy(factor.at[pl.ds(0, 16)], piv.at[0, pl.ds(0, 16)], own_sem.at[0])
         local.start()
         local.wait()
 
@@ -217,7 +221,7 @@
         return remote(
             piv.at[0, rows16],
             piv.at[(4 - k) % 4, rows16],
-            p2_send.at[k, z_other],
+            p2_send,
             p2_recv.at[(4 - k) % 4],
             wide_of(x, y, z_other, core),
             rem4(n + k),
@@ -230,7 +234,7 @@
         for k, z_other in others:
             along_z(k, z_other).start()
         for k in (2, 1, 3):
-            trade(k, 1).start()
+            trade(k, 2).start()
 
     def piece(kind, first, count):
         if kind == 0:
@@ -272,10 +276,11 @@
     def _():
         pltpu.make_async_copy(piv.at[0, rows16], piv.at[0, rows16], p2_recv.at[0]).wait()
 
-    f_copies = {k: trade(k, 0) for k in (2, 1, 3)}
-    c_copies = {k: trade(k, 1) for k in (2, 1, 3)}
-    for k in (2, 1, 3):
-        f_copies[k].start()
+    f_copies = {(k, half): trade(k, half) for k in (2, 1, 3) for half in range(2)}
+    c_copies = {k: trade(k, 2) for k in (2, 1, 3)}
+    for half in range(2):
+        for k in (2, 1, 3):
+            f_copies[k, half].start()
     first_p = gather_first(2)
 
     second, core_copies = [], []
@@ -302,13 +307,13 @@
 
     @pl.when(wide == OWNER)
     def _():
-        for to in range(1, PLANE):
-            to_plane(to).wait_send()
+        sent = piv.at[0, pl.ds(0, 16 * (PLANE - 1))]
+        pltpu.make_async_copy(sent, sent, p1_send).wait()
 
     @pl.when(z == 1)
     def _():
-        for k, z_other in others:
-            along_z(k, z_other).wait_send()
+        sent = piv.at[0, pl.ds(0, 16 * (Z * NARROW - 1))]
+        pltpu.make_async_copy(sent, sent, p2_send).wait()
 
     for k in range(NARROW):
         piv_split[0, k], piv_split[1, k] = split(piv[k])
@@ -316,92 +321,87 @@
         for which in range(2):
             dv_split[0, which, k], dv_split[1, which, k] = split(dv[which, k])
 
-    product = jnp.zeros((128, 512), jnp.float32)
-    sums = jnp.zeros((128, 512), jnp.float32)
-    squares = jnp.zeros((128, 1), jnp.float32)
-    for k in (0, 1, 3, 2):
-        if k:
-            f_copies[4 - k].wait_recv()
-        part = f_rows[k]
-        squares = squares + jnp.sum(part * part, axis=1, keepdims=True)
-        part = split(part)
-        product = product + dot3(part, (piv_split[0, k], piv_split[1, k]), 1, 1)
-        sums = sums + dot3(part, (d1_split[0, k], d1_split[1, k]), 1, 0)
-    for k in (1, 3, 2):
-        c_copies[k].wait_recv()
-    for m in range(NARROW):
-        updated[:, 128 * m : 128 * m + 128] = c_rows[m] - product[:, 128 * m : 128 * m + 128]
-    new = split(updated[...])
     inverse_split = tuple(dv_split[part, 1].reshape(512, 512) for part in range(2))
     draws_split = tuple(dv_split[part, 0].reshape(512, 512) for part in range(2))
-    value = dot3(new, inverse_split, 1, 1)
-    for k in range(NARROW):
-        panel[k] = value[:, 128 * k : 128 * k + 128]
-    squares = squares + jnp.sum(value * value, axis=1, keepdims=True)
-    sums = sums + dot3(split(value), draws_split, 1, 0)
-    scaled = sums * lax.rsqrt(squares + 1e-06)
-    uniforms = 0.5 * (1.0 + lax.erf(scaled * HALF_ROOT))
+    q_copies = {
+        (k, half): remote(
+            panel.at[k, pl.ds(64 * half, 64)],
+            panel_out.at[pl.ds(128 * n + 64 * half, 64)],
+            q_send.at[k - 1, half],
+            q_recv.at[k - 1, half],
+            wide,
+            rem4(n + k),
+        )
+        for k in (1, 2, 3)
+        for half in range(2)
+    }
+    for half in range(2):
+        rows = pl.ds(64 * half, 64)
+        product = jnp.zeros((64, 512), jnp.float32)
+        sums = jnp.zeros((64, 512), jnp.float32)
+        squares = jnp.zeros((64, 1), jnp.float32)
+        for k in (0, 1, 3, 2):
+            if k:
+                f_copies[4 - k, half].wait_recv()
+            if half and k == 2:
+                q_copies[2, 0].start()
+            part = f_rows[k, rows]
+            squares = squares + jnp.sum(part * part, axis=1, keepdims=True)
+            part = split(part)
+            product = product + dot3(part, (piv_split[0, k], piv_split[1, k]), 1, 1)
+            sums = sums + dot3(part, (d1_split[0, k], d1_split[1, k]), 1, 0)
+        if half == 0:
+            for k in (1, 3, 2):
+                c_copies[k].wait_recv()
+        for m in range(NARROW):
+            updated[:, 128 * m : 128 * m + 128] = c_rows[m, rows] - product[:, 128 * m : 128 * m + 128]
+        value = dot3(split(updated[...]), inverse_split, 1, 1)
+        for k in range(NARROW):
+            panel[k, rows] = value[:, 128 * k : 128 * k + 128]
+        squares = squares + jnp.sum(value * value, axis=1, keepdims=True)
+        sums = sums + dot3(split(value), draws_split, 1, 0)
+        scaled = sums * lax.rsqrt(squares + 1e-06)
+        flat_uni[rows, :] = 0.5 * (1.0 + lax.erf(scaled * HALF_ROOT))
     for m in range(NARROW):
-        uni[m] = uniforms[:, 128 * m : 128 * m + 128].T.reshape(X * Y, Z, CORES, 1, 128)
+        uni[m] = flat_uni[:, 128 * m : 128 * m + 128].T.reshape(X * Y, Z, CORES, 1, 128)
 
     def up(step, carry):
         to, to_n, to_z, to_wide = in_ring(lax.rem(7 * step, Z * NARROW))
         remote(
-            uni.at[to_n, :, to_z], mixed.at[:, :, z, n], u_send.at[to], u_recv.at[height], to_wide, to_n
+            uni.at[to_n, :, to_z], mixed.at[:, :, z, n], u_send, u_recv, to_wide, to_n
         ).start()
         return carry
 
     lax.fori_loop(1, Z * NARROW, up, 0)
-    q_copies = {
-        k: remote(
-            panel.at[k], panel_out.at[pl.ds(128 * n, 128)], q_send.at[k - 1], q_recv.at[k - 1], wide, rem4(n + k)
-        )
-        for k in (1, 2, 3)
-    }
-    q_copies[1].start()
-    q_copies[3].start()
+    q_copies[2, 1].start()
     local = pltpu.make_async_copy(uni.at[n, :, z], mixed.at[:, :, z, n], own_sem.at[0])
     local.start()
     kept = pltpu.make_async_copy(panel.at[0], panel_out.at[pl.ds(128 * n, 128)], own_sem.at[2])
     kept.start()
     local.wait()
 
-    def up_done(step, carry):
-        to, to_n, to_z, to_wide = in_ring(step)
-        copy = remote(
-            uni.at[to_n, :, to_z], mixed.at[:, :, to_z, to_n], u_send.at[to], u_recv.at[to], to_wide, to_n
-        )
-        copy.wait()
-        return carry
-
-    lax.fori_loop(1, Z * NARROW, up_done, 0)
+    moved = mixed.at[pl.ds(0, Z * NARROW - 1)]
+    pltpu.make_async_copy(moved, moved, u_recv).wait()
+    pltpu.make_async_copy(moved, moved, u_send).wait()
 
     def hand_out(step, carry):
         to, to_column, to_core, to_wide = in_plane(step)
         remote(
-            mixed.at[to_column, to_core], full.at[column, :, core], a_send.at[to], a_recv.at[flat], to_wide, n
+            mixed.at[to_column, to_core], full.at[column, :, core], a_send, a_recv, to_wide, n
         ).start()
         return carry
 
     lax.fori_loop(1, PLANE, hand_out, 0)
-    q_copies[2].start()
+    for half in range(2):
+        for k in (1, 3):
+            q_copies[k, half].start()
     local = pltpu.make_async_copy(mixed.at[column, core], full.at[column, :, core], own_sem.at[1])
     local.start()
     local.wait()
 
-    def handed(step, carry):
-        to, to_column, to_core, to_wide = in_plane(step)
-        remote(
-            mixed.at[to_column, to_core],
-            full.at[to_column, :, to_core],
-            a_send.at[to],
-            a_recv.at[to],
-            to_wide,
-            n,
-        ).wait()
-        return carry
-
-    lax.fori_loop(1, PLANE, handed, 0)
+    moved = piv.at[0, pl.ds(0, 8 * (PLANE - 1))]
+    pltpu.make_async_copy(moved, moved, a_recv).wait()
+    pltpu.make_async_copy(moved, moved, a_send).wait()
 
     now = full[...].reshape(512, 128)
     row = lax.broadcasted_iota(jnp.int32, (512, 128), 0)
@@ -413,16 +413,12 @@
         left = jnp.where(lane < shift, pltpu.roll(before, shift, 1), pltpu.roll(now, shift, 1))
         right = jnp.where(lane >= 128 - shift, pltpu.roll(after, 128 - shift, 1), pltpu.roll(now, 128 - shift, 1))
         total = total + weight * (left + right)
-    result[...] = total
-    done = pltpu.make_async_copy(result, smooth_out, own_sem.at[3])
-    done.start()
-    for k in (1, 2, 3):
-        f_copies[k].wait_send()
-        c_copies[k].wait_send()
-    for k in (1, 2, 3):
-        q_copies[k].wait()
+    smooth_out[...] = total
+    for copy in (*f_copies.values(), *c_copies.values()):
+        copy.wait_send()
+    for copy in q_copies.values():
+        copy.wait()
     kept.wait()
-    done.wait()
 
 
 def per_device(corr_panel, factor_prev, draws_prev, draws_panel, diag_inverse):
@@ -436,7 +432,7 @@
             jax.ShapeDtypeStruct((512, 128), jnp.float32),
         ),
         in_specs=[anywhere] * 5,
-        out_specs=(anywhere, anywhere),
+        out_specs=(pl.BlockSpec(memory_space=pltpu.VMEM), pl.BlockSpec(memory_space=pltpu.VMEM)),
         scratch_shapes=[
             pltpu.VMEM((4, 128, 256), jnp.float32),
             pltpu.VMEM((4, 128, 128), jnp.float32),
@@ -446,6 +442,7 @@
             pltpu.VMEM((2, 4, 256, 512), jnp.bfloat16),
             pltpu.VMEM((2, 2, 4, 128, 512), jnp.bfloat16),
             pltpu.VMEM((2, 4, 512, 256), jnp.bfloat16),
+            pltpu.VMEM((64, 512), jnp.float32),
             pltpu.VMEM((128, 512), jnp.float32),
             pltpu.VMEM((4, 128, 128), jnp.float32),
             pltpu.VMEM((4, X * Y, Z, CORES, 1, 128), jnp.float32),
@@ -455,29 +452,29 @@
             dma((5,)),
             dma((3, 2)),
             dma((3, 2)),
-            dma((PLANE,)),
-            dma,
-            dma((4, 4)),
+            dma,
+            dma,
+            dma,
             dma((4,)),
+            dma((3, 3)),
+            dma((3, 3)),
+            dma((3, 3)),
+            dma((3, 3)),
+            dma((3, 3)),
+            dma((3, 3)),
+            dma((4, 3)),
+            dma((4, 3)),
             dma((3, 2)),
             dma((3, 2)),
-            dma((3, 3)),
-            dma((3, 3)),
-            dma((3, 3)),
-            dma((3, 3)),
-            dma((4, 3)),
-            dma((4, 3)),
-            dma((3,)),
-            dma((3,)),
-            dma((16,)),
-            dma((16,)),
-            dma((PLANE,)),
-            dma((PLANE,)),
+            dma,
+            dma,
+            dma,
+            dma,
         ],
         compiler_params=pltpu.CompilerParams(
-            collective_id=0, has_side_effects=True, vmem_limit_bytes=67043328
+            collective_id=0, has_side_effects=True, vmem_limit_bytes=40 * 2**20
         ),
-    )(corr_panel, factor_prev, draws_prev, draws_panel, diag_inverse)
+    )(*(pltpu.with_memory_space_constraint(v, pltpu.HBM) for v in (corr_panel, factor_prev, draws_prev, draws_panel, diag_inverse)))
     return panel_factor, smoothed.reshape(1, 512 * 128)
 
 

time: 99.9 us -> 96.5 us (0.966)
  Pallas kernels: 96 us -> 94.3 us
  local copies, waits for them, and re-layouts: 2.42 us -> 1.41 us
    pallas_call x1, Pallas kernels: 96 us -> 94.3 us  [per_device(): pl.pallas_call(kernel, name='panel', out_shape=(jax.ShapeDtypeStruct((512...]
    unnamed x4 -> x2, local copies, waits for them, and re-layouts: 2.42 us -> 1.41 us
where the time goes in v4:
time: 96.5 us; the launch traced here: 96.3 us
  Pallas kernels  94.3 us (98%)
  local copies, waits for them, and re-layouts  1.41 us (1%)
    pallas_call x1, Pallas kernels, per_device(): pl.pallas_call(kernel, name='panel', out_shape=(jax.ShapeDtypeStruct((512...  94.3 us

profile of v4, /device:TPU:1, one launch (start us, length us, event | category | flops | bytes accessed | tf_op | source)
XLA Modules:
  0.0 96.3 jit_solution(10655606947730745058)
XLA Ops:
  0.6 94.3 %panel.1 = (f32[512,128]{1,0:T(8,128)S(1)}, f32[512,128]{1,0:T(8,128)S(1)}) custom-call(f32[512,128]{1,0:T(8,128)} %corr.1, f32[512,256]{1,0:T(8,128)} %factor.1, f32[256,512]{1,0:T(8,128)} %draws_prev.1, f32[128,512]{1,0:T(8,128)} %draws_panel.1, f32[128,512]{1,0:T(8,128)} %inverse.1), custom_call_target="tpu_custom_call" | custom-call | tf_op jit(solution)/shard_map/panel/pallas_call | solution.py:427
  94.9 0.7 copy.9
  95.6 0.7 copy.10

commit v5 on v4

--- a/solution.py
+++ b/solution.py
@@ -71,6 +71,8 @@
     own_sem,
     d_send,
     d_recv,
+    z_send,
+    z_recv,
     p1_send,
     p1_recv,
     p2_send,
@@ -81,6 +83,8 @@
     g1_recv,
     g2_send,
     g2_recv,
+    g3_send,
+    g3_recv,
     x_send,
     x_recv,
     q_send,
@@ -159,29 +163,15 @@
     rows8 = pl.ds(8 * place, 8)
     rows8_core = pl.ds(8 * (4 * a + b), 8)
     rows16 = pl.ds(16 * place, 16)
+    quarter = pl.ds(pl.multiple_of(128 * z, 128), 128)
     d_copies = []
     for k in (2, 1, 3):
-        peer = rem4(n + k)
-        d_copies.append(
-            send(
-                d1.at[0, rows8],
-                d1.at[4 - k, rows8],
-                d_send.at[k - 1, 0],
-                d_recv.at[k - 1, 0],
-                wide,
-                peer,
+        for kind, ref in enumerate((d1.at[:, rows8, quarter], dv.at[core, :, rows8_core, quarter])):
+            d_copies.append(
+                send(
+                    ref.at[0], ref.at[4 - k], d_send.at[k - 1, kind], d_recv.at[k - 1, kind], wide, rem4(n + k)
+                )
             )
-        )
-        d_copies.append(
-            send(
-                dv.at[core, 0, rows8_core],
-                dv.at[core, 4 - k, rows8_core],
-                d_send.at[k - 1, 1],
-                d_recv.at[k - 1, 1],
-                wide,
-                peer,
-            )
-        )
 
     def trade(k, kind):
         peer = rem4(n + k)
@@ -194,8 +184,7 @@
 
     @pl.when(z != 1)
     def _():
-        for k in (2, 1, 3):
-            trade(k, 2).start()
+        trade(2, 2).start()
 
     def to_plane(to):
         to_core, to_a, to_b = to // 16, (to // 4) % 4, to % 4
@@ -233,8 +222,7 @@
     def _():
         for k, z_other in others:
             along_z(k, z_other).start()
-        for k in (2, 1, 3):
-            trade(k, 2).start()
+        trade(2, 2).start()
 
     def piece(kind, first, count):
         if kind == 0:
@@ -261,13 +249,27 @@
 
     def gather_second(kind):
         ref = piece(kind, 16 * core + 4 * a, 4)
-        return [
-            send(ref, ref, g2_send.at[step - 1, kind], g2_recv.at[step - 1, kind], along(step, 1 - core), n)
-            for step in (1, 3, 2)
-        ]
+        return {
+            step: send(ref, ref, g2_send.at[step // 2, kind], g2_recv.at[step // 2, kind], along(step, 1 - core), n)
+            for step in (1, 3)
+        }
+
+    def pass_on(kind, step):
+        group, half = rem4(a + 4 - step), step // 2
+        ref = piece(kind, 16 * core + 4 * group + 2 * half, 2)
+        return send(ref, ref, g3_send.at[half, kind], g3_recv.at[half, kind], along(step, 1 - core), n)
 
     for copy in d_copies:
         copy.wait_recv()
+    z_copies = []
+    for step in (1, 2, 3):
+        to_wide = wide_of(x, y, rem4(z + step), core)
+        for kind, ref in enumerate((d1.at[pl.ds(1, 3), rows8, quarter], dv.at[core, pl.ds(1, 3), rows8_core, quarter])):
+            z_copies.append(send(ref, ref, z_send.at[step - 1, kind], z_recv.at[step - 1, kind], to_wide, n))
+    trade(1, 2).start()
+    trade(3, 2).start()
+    for copy in z_copies:
+        copy.wait()
     first_d = [gather_first(0), gather_first(1)]
     for slot in range(1, NARROW):
         pltpu.make_async_copy(piv.at[slot, rows16], piv.at[slot, rows16], p2_recv.at[slot]).wait()
@@ -293,15 +295,23 @@
         copy.wait()
     second.append(gather_second(2))
     core_copies.append(to_partner(2, a, 0))
+    third = []
     for kind in range(3):
-        for order, step in enumerate((1, 3, 2)):
-            second[kind][order].wait_recv()
+        for step in (1, 3):
+            second[kind][step].wait_recv()
+            third.append(pass_on(kind, step))
             core_copies.append(to_partner(kind, rem4(a + 4 - step), step))
+    for kind in range(3):
+        third[2 * kind].wait_recv()
+        third[2 * kind + 1].wait_recv()
+        core_copies.append(to_partner(kind, rem4(a + 2), 2))
     for copy in d_copies:
         copy.wait_send()
     for copies in second:
-        for copy in copies:
-            copy.wait_send()
+        copies[1].wait_send()
+        copies[3].wait_send()
+    for copy in third:
+        copy.wait_send()
     for copy in core_copies:
         copy.wait()
 
@@ -452,6 +462,8 @@
             dma((5,)),
             dma((3, 2)),
             dma((3, 2)),
+            dma((3, 2)),
+            dma((3, 2)),
             dma,
             dma,
             dma,
@@ -460,8 +472,10 @@
             dma((3, 3)),
             dma((3, 3)),
             dma((3, 3)),
-            dma((3, 3)),
-            dma((3, 3)),
+            dma((2, 3)),
+            dma((2, 3)),
+            dma((2, 3)),
+            dma((2, 3)),
             dma((4, 3)),
             dma((4, 3)),
             dma((3, 2)),

time: 96.5 us -> 94.7 us (0.981)
  Pallas kernels: 94.3 us -> 92.5 us
    pallas_call x1, Pallas kernels: 94.3 us -> 92.5 us  [per_device(): pl.pallas_call(kernel, name='panel', out_shape=(jax.ShapeDtypeStruct((512...]
where the time goes in v5:
time: 94.7 us; the launch traced here: 94.5 us
  Pallas kernels  92.5 us (98%)
  local copies, waits for them, and re-layouts  1.41 us (1%)
    pallas_call x1, Pallas kernels, per_device(): pl.pallas_call(kernel, name='panel', out_shape=(jax.ShapeDtypeStruct((512...  92.5 us

profile of v5, /device:TPU:1, one launch (start us, length us, event | category | flops | bytes accessed | tf_op | source)
XLA Modules:
  0.0 94.5 jit_solution(366141781510714905)
XLA Ops:
  0.6 92.5 %panel.1 = (f32[512,128]{1,0:T(8,128)S(1)}, f32[512,128]{1,0:T(8,128)S(1)}) custom-call(f32[512,128]{1,0:T(8,128)} %corr.1, f32[512,256]{1,0:T(8,128)} %factor.1, f32[256,512]{1,0:T(8,128)} %draws_prev.1, f32[128,512]{1,0:T(8,128)} %draws_panel.1, f32[128,512]{1,0:T(8,128)} %inverse.1), custom_call_target="tpu_custom_call" | custom-call | tf_op jit(solution)/shard_map/panel/pallas_call | solution.py:437
  93.1 0.7 copy.9
  93.8 0.7 copy.10

commit v6 on v5

--- a/solution.py
+++ b/solution.py
@@ -383,7 +383,6 @@
         return carry
 
     lax.fori_loop(1, Z * NARROW, up, 0)
-    q_copies[2, 1].start()
     local = pltpu.make_async_copy(uni.at[n, :, z], mixed.at[:, :, z, n], own_sem.at[0])
     local.start()
     kept = pltpu.make_async_copy(panel.at[0], panel_out.at[pl.ds(128 * n, 128)], own_sem.at[2])
@@ -402,6 +401,7 @@
         return carry
 
     lax.fori_loop(1, PLANE, hand_out, 0)
+    q_copies[2, 1].start()
     for half in range(2):
         for k in (1, 3):
             q_copies[k, half].start()

time: 94.7 us -> 95.1 us (level)
  no operation moved by 1% of the time
where the time goes in v6:
time: 95.1 us; the launch traced here: 94.2 us
  Pallas kernels  92.1 us (97%)
  local copies, waits for them, and re-layouts  1.41 us (1%)
    pallas_call x1, Pallas kernels, per_device(): pl.pallas_call(kernel, name='panel', out_shape=(jax.ShapeDtypeStruct((512...  92.1 us

profile of v6, /device:TPU:1, one launch (start us, length us, event | category | flops | bytes accessed | tf_op | source)
XLA Modules:
  0.0 94.2 jit_solution(9463839614389532550)
XLA Ops:
  0.6 92.1 %panel.1 = (f32[512,128]{1,0:T(8,128)S(1)}, f32[512,128]{1,0:T(8,128)S(1)}) custom-call(f32[512,128]{1,0:T(8,128)} %corr.1, f32[512,256]{1,0:T(8,128)} %factor.1, f32[256,512]{1,0:T(8,128)} %draws_prev.1, f32[128,512]{1,0:T(8,128)} %draws_panel.1, f32[128,512]{1,0:T(8,128)} %inverse.1), custom_call_target="tpu_custom_call" | custom-call | tf_op jit(solution)/shard_map/panel/pallas_call | solution.py:437
  92.8 0.7 copy.9
  93.5 0.7 copy.10
